TPU v7x, 512 devices: a whole 4x8x8 slice. The times are simulated.
512 devices in a mesh: dp: 8 (over z), expert: 64 (over y, x, core).
Axes of the slice: x: 4, y: 8, z: 8, core: 2. Of those that a mesh axis runs over, the one named last changes fastest.
Arguments:
- tokens: bfloat16 [65536, 3584], P(('dp', 'expert')), may hold values from -6 to 6
- cotangent: bfloat16 [65536, 3584], P(('dp', 'expert')), may hold values from -6 to 6
- route_ids: int32 [65536, 8], P(('dp', 'expert')), may hold values from 0 to 255, as said below
- route_gates: float32 [65536, 8], P(('dp', 'expert')), may hold values from 0.1 to 1
- gate_w: bfloat16 [3584, 8192], P('dp', 'expert'), may hold values from -0.09375 to 0.09375
- up_w: bfloat16 [3584, 8192], P('dp', 'expert'), may hold values from -0.09375 to 0.09375
- down_w: bfloat16 [3584, 8192], P('dp', 'expert'), may hold values from -0.1875 to 0.1875
Outputs:
- moe_out: bfloat16 [65536, 3584], P(('dp', 'expert'))
- d_tokens: bfloat16 [65536, 3584], P(('dp', 'expert'))
- d_gates: float32 [65536, 8], P(('dp', 'expert'))
- d_gate_w: bfloat16 [3584, 8192], P('dp', 'expert')
- d_up_w: bfloat16 [3584, 8192], P('dp', 'expert')
- d_down_w: bfloat16 [3584, 8192], P('dp', 'expert')
Inputs may be any that keep to these rules, and one draw needn't show every extreme that they name: `route_ids`: each token names 8 different experts; the experts in flight are 0 to 7. Among the tokens of one device (aligned blocks of 128 tokens) each expert in flight is named by at most 6 tokens, and in every draw one expert in flight is named by exactly 6 tokens in every block.
All inputs are finite; a program needn't handle non-finite values.
Results may differ from a plain program's by a relative error of at most 0.017.
Values may be sent and summed in bfloat16 or wider, within the bound.
A program may use at most 64 MiB of HBM per device.

v0:
```python
import jax
import jax.numpy as jnp
from jax import lax
from jax.sharding import PartitionSpec as P

TOP = 8
SLICES = 8
CAP = 6


def shards(tokens, cotangent, route_ids, route_gates, gate_w, up_w, down_w):
    owners = lax.axis_size("expert")
    groups = owners // SLICES
    tok_rows = tokens.shape[0]
    routes = tok_rows * TOP
    flat_ids = route_ids.reshape(routes)
    matched = (flat_ids[:, None] == jnp.arange(groups, dtype=jnp.int32)[None, :]).astype(jnp.int32)
    slot_index = jnp.cumsum(matched, axis=0) - 1
    chosen = (matched[:, :, None] == 1) & (
        slot_index[:, :, None] == jnp.arange(CAP, dtype=jnp.int32)[None, None, :]
    )
    select = jnp.transpose(chosen, (1, 2, 0)).reshape(groups * CAP, routes).astype(jnp.float32)
    tok_select = jnp.sum(select.reshape(groups * CAP, tok_rows, TOP), axis=2)
    slot_gate = jnp.sum(select * route_gates.reshape(routes)[None, :], axis=1)
    pick_rows = tok_select.astype(jnp.bfloat16)
    token_slots = jnp.dot(pick_rows, tokens, preferred_element_type=jnp.float32).astype(
        jnp.bfloat16
    )
    cotangent_slots = jnp.dot(pick_rows, cotangent, preferred_element_type=jnp.float32).astype(
        jnp.bfloat16
    )
    scaled_slots = (slot_gate[:, None] * cotangent_slots.astype(jnp.float32)).astype(jnp.bfloat16)

    def spread(slot_rows):
        width = slot_rows.shape[1]
        grouped = slot_rows.reshape(groups, 1, CAP, width)
        return jnp.broadcast_to(grouped, (groups, SLICES, CAP, width)).reshape(owners * CAP, width)

    w_gate, w_up, w_down = (
        lax.all_gather(gate_w, "dp", axis=0, tiled=True),
        lax.all_gather(up_w, "dp", axis=0, tiled=True),
        lax.all_gather(down_w, "dp", axis=0, tiled=True),
    )
    token_rows = lax.all_to_all(
        spread(token_slots), "expert", split_axis=0, concat_axis=0, tiled=True
    )
    gate_pre = jnp.dot(token_rows, w_gate, preferred_element_type=jnp.float32)
    up_pre = jnp.dot(token_rows, w_up, preferred_element_type=jnp.float32)
    sigmoid_gate = jax.nn.sigmoid(gate_pre)
    active = gate_pre * sigmoid_gate
    hidden = (active * up_pre).astype(jnp.bfloat16)
    contract_cols = (((1,), (1,)), ((), ()))
    out_part = lax.dot_general(
        hidden, w_down, contract_cols, preferred_element_type=jnp.float32
    ).astype(jnp.bfloat16)
    out_back = lax.all_to_all(out_part, "expert", split_axis=0, concat_axis=0, tiled=True)
    scaled_rows = lax.all_to_all(
        spread(scaled_slots), "expert", split_axis=0, concat_axis=0, tiled=True
    )
    d_hidden = jnp.dot(scaled_rows, w_down, preferred_element_type=jnp.float32)
    d_gate_pre = (
        d_hidden * up_pre * sigmoid_gate * (1.0 + gate_pre * (1.0 - sigmoid_gate))
    ).astype(jnp.bfloat16)
    d_up_pre = (d_hidden * active).astype(jnp.bfloat16)
    dx_part = lax.dot_general(d_gate_pre, w_gate, contract_cols, preferred_element_type=jnp.float32)
    dx_part = (
        dx_part + lax.dot_general(d_up_pre, w_up, contract_cols, preferred_element_type=jnp.float32)
    ).astype(jnp.bfloat16)
    contract_rows = (((0,), (0,)), ((), ()))
    gate_term = lax.dot_general(
        token_rows, d_gate_pre, contract_rows, preferred_element_type=jnp.float32
    )
    up_term = lax.dot_general(
        token_rows, d_up_pre, contract_rows, preferred_element_type=jnp.float32
    )
    down_term = lax.dot_general(
        scaled_rows, hidden, contract_rows, preferred_element_type=jnp.float32
    )
    summed_grads = lax.psum_scatter(
        jnp.concatenate([gate_term, up_term, down_term], axis=1).astype(jnp.bfloat16),
        "dp",
        scatter_dimension=0,
        tiled=True,
    ).astype(jnp.float32)
    hidden_cols = gate_w.shape[1]
    d_gate_w = summed_grads[:, :hidden_cols].astype(jnp.bfloat16)
    d_up_w = summed_grads[:, hidden_cols : 2 * hidden_cols].astype(jnp.bfloat16)
    d_down_w = summed_grads[:, 2 * hidden_cols :].astype(jnp.bfloat16)
    dx_back = lax.all_to_all(dx_part, "expert", split_axis=0, concat_axis=0, tiled=True)
    member_wide = spread(tok_select)
    weighted_wide = spread(tok_select * slot_gate[:, None])
    weight_high = weighted_wide.astype(jnp.bfloat16)
    weight_low = (weighted_wide - weight_high.astype(jnp.float32)).astype(jnp.bfloat16)
    moe_sum = lax.dot_general(
        weight_high, out_back, contract_rows, preferred_element_type=jnp.float32
    )
    moe_sum = moe_sum + lax.dot_general(
        weight_low, out_back, contract_rows, preferred_element_type=jnp.float32
    )
    moe_out = moe_sum.astype(jnp.bfloat16)
    d_tokens = lax.dot_general(
        member_wide.astype(jnp.bfloat16), dx_back, contract_rows, preferred_element_type=jnp.float32
    ).astype(jnp.bfloat16)
    inner = lax.dot_general(cotangent, out_back, contract_cols, preferred_element_type=jnp.float32)
    wide_grad = jnp.sum(inner * jnp.transpose(member_wide), axis=0)
    slot_grad = jnp.sum(wide_grad.reshape(groups, SLICES, CAP), axis=1).reshape(groups * CAP)
    d_gates = jnp.sum(slot_grad[:, None] * select, axis=0).reshape(tok_rows, TOP)
    return (moe_out, d_tokens, d_gates, d_gate_w, d_up_w, d_down_w)


def solution(mesh):
    return jax.shard_map(
        shards,
        mesh=mesh,
        in_specs=(
            P(("dp", "expert"), None),
            P(("dp", "expert"), None),
            P(("dp", "expert"), None),
            P(("dp", "expert"), None),
            P("dp", "expert"),
            P("dp", "expert"),
            P("dp", "expert"),
        ),
        out_specs=(
            P(("dp", "expert"), None),
            P(("dp", "expert"), None),
            P(("dp", "expert"), None),
            P("dp", "expert"),
            P("dp", "expert"),
            P("dp", "expert"),
        ),
        check_vma=False,
    )
```

profile of v0, /device:TPU:2, one launch (start us, length us, event | category | flops | bytes accessed | tf_op | source)
XLA Modules:
  0.0 461.1 jit_solution(1026153735217437292)
XLA Ops:
  13.2 3.4 eq.81
  16.6 2.9 convert_reduce_fusion
  22.1 11.0 %all-to-all-start = ((bf16[64,6,3584]{2,1,0:T(8,128)(2,1)}), bf16[64,6,3584]{2,1,0:T(8,128)(2,1)}, u32[]{:S(2)}, u32[]{:S(2)}) async-start(bf16[64,6,3584]{2,1,0:T(8,128)(2,1)} %bitcast.37), calls=%async_computation | async-start | bytes 7340032 | tf_op jit(solution)/shard_map/all_to_all | solution.py:44
  33.1 32.2 %all_gather.9 = bf16[3584,128]{1,0:T(8,128)(2,1)S(1)} all-gather(bf16[448,128]{1,0:T(8,128)(2,1)S(1)} %copy-done.10), channel_id=1, replica_groups=mesh['dp'=8,'expert'=64] {'dp'}, dimensions={0}, use_global_device_ids=true | all-gather | bytes 1032192 | tf_op jit(solution)/shard_map/all_gather | solution.py:40
  65.3 26.5 %all_gather.10 = bf16[3584,128]{1,0:T(8,128)(2,1)S(1)} all-gather(bf16[448,128]{1,0:T(8,128)(2,1)S(1)} %copy-done.11), channel_id=1, replica_groups=mesh['dp'=8,'expert'=64] {'dp'}, dimensions={0}, use_global_device_ids=true | all-gather | bytes 1032192 | tf_op jit(solution)/shard_map/all_gather | solution.py:41
  91.8 28.6 %all_gather.11 = bf16[3584,128]{1,0:T(8,128)(2,1)} all-gather(bf16[448,128]{1,0:T(8,128)(2,1)S(1)} %copy-done.12), channel_id=1, replica_groups=mesh['dp'=8,'expert'=64] {'dp'}, dimensions={0}, use_global_device_ids=true | all-gather | bytes 1032192 | tf_op jit(solution)/shard_map/all_gather | solution.py:42
  120.4 5.5 %all_to_all.34 = bf16[384,3584]{1,0:T(8,128)(2,1)} reshape(bf16[64,6,3584]{2,1,0:T(8,128)(2,1)} %all-to-all-done) | data formatting | bytes 5505024 | tf_op jit(solution)/shard_map/all_to_all | solution.py:44
  125.8 2.8 fusion.12
  129.8 2.5 convolution_convert_fusion
  132.3 5.4 %all_to_all.35 = bf16[64,6,3584]{2,1,0:T(8,128)(2,1)} reshape(bf16[384,3584]{1,0:T(8,128)(2,1)} %convolution_convert_fusion) | data formatting | bytes 5505024 | tf_op jit(solution)/shard_map/all_to_all | solution.py:56
  137.7 10.1 %all-to-all-start.1 = ((bf16[64,6,3584]{2,1,0:T(8,128)(2,1)}), bf16[64,6,3584]{2,1,0:T(8,128)(2,1)}, u32[]{:S(2)}, u32[]{:S(2)}) async-start(bf16[64,6,3584]{2,1,0:T(8,128)(2,1)} %all_to_all.35), calls=%async_computation.1 | async-start | bytes 7340032 | tf_op jit(solution)/shard_map/all_to_all | solution.py:56
  148.2 84.5 %all-to-all-done.1 = bf16[64,6,3584]{2,1,0:T(8,128)(2,1)} async-done(((bf16[64,6,3584]{2,1,0:T(8,128)(2,1)}), bf16[64,6,3584]{2,1,0:T(8,128)(2,1)}, u32[]{:S(2)}, u32[]{:S(2)}) %all-to-all-start.1) | async-done | bytes 2752544 | tf_op jit(solution)/shard_map/all_to_all | solution.py:56
  232.7 5.5 %all_to_all.37 = bf16[384,3584]{1,0:T(8,128)(2,1)} reshape(bf16[64,6,3584]{2,1,0:T(8,128)(2,1)} %all-to-all-done.1) | data formatting | bytes 5505024 | tf_op jit(solution)/shard_map/all_to_all | solution.py:56
  238.2 2.7 fusion.5
  242.1 90.3 %all_to_all.48 = bf16[64,6,3584]{2,1,0:T(8,128)(2,1)} all-to-all(bf16[64,6,3584]{2,1,0:T(8,128)(2,1)S(1)} %bitcast.38), channel_id=1, replica_groups=mesh['dp'=8,'expert'=64] {'expert'}, dimensions={0} | all-to-all | bytes 5505024 | tf_op jit(solution)/shard_map/all_to_all | solution.py:57
  332.4 5.5 %all_to_all.40 = bf16[384,3584]{1,0:T(8,128)(2,1)} reshape(bf16[64,6,3584]{2,1,0:T(8,128)(2,1)} %all_to_all.48) | data formatting | bytes 5505024 | tf_op jit(solution)/shard_map/all_to_all | solution.py:57
  337.9 2.6 convolution_convert_fusion.1
  347.7 5.4 %all_to_all.41 = bf16[64,6,3584]{2,1,0:T(8,128)(2,1)} reshape(bf16[384,3584]{1,0:T(8,128)(2,1)} %fusion) | data formatting | bytes 5505024 | tf_op jit(solution)/shard_map/all_to_all | solution.py:89
  353.1 5.6 %all-to-all-start.3 = ((bf16[64,6,3584]{2,1,0:T(8,128)(2,1)}), bf16[64,6,3584]{2,1,0:T(8,128)(2,1)}, u32[]{:S(2)}, u32[]{:S(2)}) async-start(bf16[64,6,3584]{2,1,0:T(8,128)(2,1)} %all_to_all.41), calls=%async_computation.3 | async-start | bytes 7340032 | tf_op jit(solution)/shard_map/all_to_all | solution.py:89
  360.4 4.5 copy.35
  368.5 3.4 fusion.1
  371.8 71.8 %all-to-all-done.3 = bf16[64,6,3584]{2,1,0:T(8,128)(2,1)} async-done(((bf16[64,6,3584]{2,1,0:T(8,128)(2,1)}), bf16[64,6,3584]{2,1,0:T(8,128)(2,1)}, u32[]{:S(2)}, u32[]{:S(2)}) %all-to-all-start.3) | async-done | bytes 2752544 | tf_op jit(solution)/shard_map/all_to_all | solution.py:89
  443.6 5.6 %all_to_all.43 = bf16[384,3584]{1,0:T(8,128)(2,1)} reshape(bf16[64,6,3584]{2,1,0:T(8,128)(2,1)} %all-to-all-done.3) | data formatting | bytes 5505024 | tf_op jit(solution)/shard_map/all_to_all | solution.py:89
  449.2 3.4 convolution_convert_fusion.4
  (81 shorter events, 25.1 us)
Async XLA Ops:
  7.2 231.1 %copy-start = (bf16[128,3584]{1,0:T(8,128)(2,1)S(1)}, bf16[128,3584]{1,0:T(8,128)(2,1)}, u32[]{:S(2)}) copy-start(bf16[128,3584]{1,0:T(8,128)(2,1)} %param.8) | copy-start | bytes 2752516
  16.6 2.9 copy-start.9
  22.0 11.0 %copy-start.10 = (bf16[448,128]{1,0:T(8,128)(2,1)S(1)}, bf16[448,128]{1,0:T(8,128)(2,1)}, u32[]{:S(2)}) copy-start(bf16[448,128]{1,0:T(8,128)(2,1)} %param.11) | copy-start | bytes 344068
  22.0 43.2 %copy-start.11 = (bf16[448,128]{1,0:T(8,128)(2,1)S(1)}, bf16[448,128]{1,0:T(8,128)(2,1)}, u32[]{:S(2)}) copy-start(bf16[448,128]{1,0:T(8,128)(2,1)} %param.12) | copy-start | bytes 344068
  22.1 69.8 %copy-start.12 = (bf16[448,128]{1,0:T(8,128)(2,1)S(1)}, bf16[448,128]{1,0:T(8,128)(2,1)}, u32[]{:S(2)}) copy-start(bf16[448,128]{1,0:T(8,128)(2,1)} %param.13) | copy-start | bytes 344068
  22.1 98.3 %all-to-all-start = ((bf16[64,6,3584]{2,1,0:T(8,128)(2,1)}), bf16[64,6,3584]{2,1,0:T(8,128)(2,1)}, u32[]{:S(2)}, u32[]{:S(2)}) async-start(bf16[64,6,3584]{2,1,0:T(8,128)(2,1)} %bitcast.37), calls=%async_computation | async-start | bytes 7340032 | tf_op jit(solution)/shard_map/all_to_all | solution.py:44
  91.8 36.8 %copy-start.5 = (bf16[3584,128]{1,0:T(8,128)(2,1)}, bf16[3584,128]{1,0:T(8,128)(2,1)S(1)}, u32[]{:S(2)}) copy-start(bf16[3584,128]{1,0:T(8,128)(2,1)S(1)} %all_gather.10) | copy-start | bytes 2752516
  125.8 2.8 copy-start.2
  128.7 1.2 copy-start.7
  137.7 10.1 %copy-start.13 = (f32[128,8]{0,1:T(8,128)S(1)}, f32[128,8]{0,1:T(8,128)}, u32[]{:S(2)}) copy-start(f32[128,8]{0,1:T(8,128)} %param.10) | copy-start | bytes 12292
  137.7 95.0 %all-to-all-start.1 = ((bf16[64,6,3584]{2,1,0:T(8,128)(2,1)}), bf16[64,6,3584]{2,1,0:T(8,128)(2,1)}, u32[]{:S(2)}, u32[]{:S(2)}) async-start(bf16[64,6,3584]{2,1,0:T(8,128)(2,1)} %all_to_all.35), calls=%async_computation.1 | async-start | bytes 7340032 | tf_op jit(solution)/shard_map/all_to_all | solution.py:56
  337.8 2.6 copy-start.4
  337.9 2.8 copy-start.8
  340.7 1.8 copy-start.3
  344.0 1.2 copy-start.6
  353.1 90.6 %all-to-all-start.3 = ((bf16[64,6,3584]{2,1,0:T(8,128)(2,1)}), bf16[64,6,3584]{2,1,0:T(8,128)(2,1)}, u32[]{:S(2)}, u32[]{:S(2)}) async-start(bf16[64,6,3584]{2,1,0:T(8,128)(2,1)} %all_to_all.41), calls=%async_computation.3 | async-start | bytes 7340032 | tf_op jit(solution)/shard_map/all_to_all | solution.py:89
  358.7 93.9 %reduce-scatter.4.cloned.1.call-start = ((), (), s32[]{:S(2)}) async-start(), calls=%async_computation.5 | async-start | bytes 3096576
  443.6 10.7 %copy-start.1 = (bf16[128,3584]{1,0:T(8,128)(2,1)S(1)}, bf16[128,3584]{1,0:T(8,128)(2,1)}, u32[]{:S(2)}) copy-start(bf16[128,3584]{1,0:T(8,128)(2,1)} %param.8) | copy-start | bytes 2752516
Sparse Core Ops, SparseCore 0:
  365.1 46.6 reduce-scatter.3
where the time goes:
time: 463 us; the launch traced here: 461 us
  blocking collectives  178 us (38%)
  waiting for transfers between devices  156 us (34%)
  local copies, waits for them, and re-layouts  51.9 us (11%)
  matrix products  26.8 us (6%)
  starting transfers between devices  26.8 us (6%)
  between operations  14.4 us (3%)
  other arithmetic  7.41 us (2%)
    all_to_all x1, blocking collectives, shards(): lax.all_to_all(spread(scaled_slots), 'expert', split_axis=0, concat_axis=...  90.3 us
    all_to_all x1, waiting for transfers between devices, shards(): lax.all_to_all(out_part, 'expert', split_axis=0, concat_axis=0, tiled=True)  84.5 us
    all_to_all x1, waiting for transfers between devices, shards(): lax.all_to_all(dx_part, 'expert', split_axis=0, concat_axis=0, tiled=True)  71.8 us
    all_gather x1, blocking collectives, shards(): lax.all_gather(gate_w, 'dp', axis=0, tiled=True)  32.2 us
    all_gather x1, blocking collectives, shards(): lax.all_gather(down_w, 'dp', axis=0, tiled=True)  28.6 us
    all_gather x1, blocking collectives, shards(): lax.all_gather(up_w, 'dp', axis=0, tiled=True)  26.5 us
    all_to_all x1, starting transfers between devices, shards(): lax.all_to_all(spread(token_slots), 'expert', split_axis=0, concat_axis=0...  11 us
    all_to_all x2, local copies, waits for them, and re-layouts, shards(): lax.all_to_all(dx_part, 'expert', split_axis=0, concat_axis=0, tiled=True)  11 us
  transfers between devices with their start and end apart: 4, of which 2 were waited for; matrix products, arithmetic and copies ran while one was open for 4% of the time, Pallas kernels for 0%

commit v1 on v0

--- a/solution.py
+++ b/solution.py
@@ -39,7 +39,9 @@
     w_gate, w_up, w_down = (
         lax.all_gather(gate_w, "dp", axis=0, tiled=True),
         lax.all_gather(up_w, "dp", axis=0, tiled=True),
-        lax.all_gather(down_w, "dp", axis=0, tiled=True),
+        jnp.concatenate(
+            lax.all_to_all(jnp.stack([down_w] * lax.axis_size("dp")), "dp", 0, 0), axis=0
+        ),
     )
     token_rows = lax.all_to_all(
         spread(token_slots), "expert", split_axis=0, concat_axis=0, tiled=True

time: 463 us -> 538 us (1.16)
  blocking collectives: 178 us -> 256 us
    all_to_all x0 -> x1, blocking collectives: none -> 95.7 us  [shards(): lax.all_to_all(spread(token_slots), 'expert', split_axis=0, concat_axis=0...]
    all_gather x1 -> x0, blocking collectives: 28.6 us -> none  [shards(): lax.all_gather(down_w, 'dp', axis=0, tiled=True)]
    all_gather x1, blocking collectives: 32.2 us -> 43.2 us  [shards(): lax.all_gather(gate_w, 'dp', axis=0, tiled=True)]
where the time goes in v1:
time: 538 us; the launch traced here: 536 us
  blocking collectives  256 us (48%)
  waiting for transfers between devices  156 us (29%)
  local copies, waits for them, and re-layouts  50.1 us (9%)
  matrix products  29.3 us (5%)
  starting transfers between devices  23 us (4%)
  between operations  14.4 us (3%)
  other arithmetic  7.4 us (1%)
    all_to_all x1, blocking collectives, shards(): lax.all_to_all(spread(token_slots), 'expert', split_axis=0, concat_axis=0...  95.7 us
    all_to_all x1, blocking collectives, shards(): lax.all_to_all(spread(scaled_slots), 'expert', split_axis=0, concat_axis=...  90.3 us
    all_to_all x1, waiting for transfers between devices, shards(): lax.all_to_all(out_part, 'expert', split_axis=0, concat_axis=0, tiled=True)  84.5 us
    all_to_all x1, waiting for transfers between devices, shards(): lax.all_to_all(dx_part, 'expert', split_axis=0, concat_axis=0, tiled=True)  71.8 us
    all_gather x1, blocking collectives, shards(): lax.all_gather(gate_w, 'dp', axis=0, tiled=True)  43.2 us
    all_gather x1, blocking collectives, shards(): lax.all_gather(up_w, 'dp', axis=0, tiled=True)  26.4 us
    all_to_all x2, local copies, waits for them, and re-layouts, shards(): lax.all_to_all(dx_part, 'expert', split_axis=0, concat_axis=0, tiled=True)  11 us
    all_to_all x2, local copies, waits for them, and re-layouts, shards(): lax.all_to_all(out_part, 'expert', split_axis=0, concat_axis=0, tiled=True)  10.9 us
  transfers between devices with their start and end apart: 4, of which 2 were waited for; matrix products, arithmetic and copies ran while one was open for 4% of the time, Pallas kernels for 0%

profile of v1, /device:TPU:2, one launch (start us, length us, event | category | flops | bytes accessed | tf_op | source)
XLA Modules:
  0.0 536.1 jit_solution(15645151735259346076)
XLA Ops:
  13.2 3.4 eq.81
  16.6 2.9 convert_reduce_fusion
  20.2 95.7 %all_to_all.53 = bf16[64,6,3584]{2,1,0:T(8,128)(2,1)} all-to-all(bf16[64,6,3584]{2,1,0:T(8,128)(2,1)S(1)} %bitcast.38), channel_id=1, replica_groups=mesh['dp'=8,'expert'=64] {'expert'}, dimensions={0} | all-to-all | bytes 5505024 | tf_op jit(solution)/shard_map/all_to_all | solution.py:46
  116.9 10.3 %all-to-all-start.1 = ((bf16[8,448,128]{2,1,0:T(8,128)(2,1)}), bf16[8,448,128]{2,1,0:T(8,128)(2,1)}, u32[]{:S(2)}, u32[]{:S(2)}) async-start(bf16[8,448,128]{2,1,0:T(8,128)(2,1)} %stack.2), calls=%async_computation.1 | async-start | bytes 1835008 | tf_op jit(solution)/shard_map/all_to_all | solution.py:43
  127.3 43.2 %all_gather.6 = bf16[3584,128]{1,0:T(8,128)(2,1)S(1)} all-gather(bf16[448,128]{1,0:T(8,128)(2,1)S(1)} %copy-done.9), channel_id=1, replica_groups=mesh['dp'=8,'expert'=64] {'dp'}, dimensions={0}, use_global_device_ids=true | all-gather | bytes 1032192 | tf_op jit(solution)/shard_map/all_gather | solution.py:40
  170.5 26.4 %all_gather.7 = bf16[3584,128]{1,0:T(8,128)(2,1)S(1)} all-gather(bf16[448,128]{1,0:T(8,128)(2,1)S(1)} %copy-done.10), channel_id=1, replica_groups=mesh['dp'=8,'expert'=64] {'dp'}, dimensions={0}, use_global_device_ids=true | all-gather | bytes 1032192 | tf_op jit(solution)/shard_map/all_gather | solution.py:41
  196.9 5.8 %all_to_all.37 = bf16[384,3584]{1,0:T(8,128)(2,1)} reshape(bf16[64,6,3584]{2,1,0:T(8,128)(2,1)} %all_to_all.53) | data formatting | bytes 5505024 | tf_op jit(solution)/shard_map/all_to_all | solution.py:46
  202.7 2.8 fusion.12
  206.4 3.6 convolution_convert_fusion
  210.0 5.4 %all_to_all.39 = bf16[64,6,3584]{2,1,0:T(8,128)(2,1)} reshape(bf16[384,3584]{1,0:T(8,128)(2,1)} %convolution_convert_fusion) | data formatting | bytes 5505024 | tf_op jit(solution)/shard_map/all_to_all | solution.py:58
  215.4 7.0 %all-to-all-start.2 = ((bf16[64,6,3584]{2,1,0:T(8,128)(2,1)}), bf16[64,6,3584]{2,1,0:T(8,128)(2,1)}, u32[]{:S(2)}, u32[]{:S(2)}) async-start(bf16[64,6,3584]{2,1,0:T(8,128)(2,1)} %all_to_all.39), calls=%async_computation.2 | async-start | bytes 7340032 | tf_op jit(solution)/shard_map/all_to_all | solution.py:58
  222.9 84.5 %all-to-all-done.2 = bf16[64,6,3584]{2,1,0:T(8,128)(2,1)} async-done(((bf16[64,6,3584]{2,1,0:T(8,128)(2,1)}), bf16[64,6,3584]{2,1,0:T(8,128)(2,1)}, u32[]{:S(2)}, u32[]{:S(2)}) %all-to-all-start.2) | async-done | bytes 2752544 | tf_op jit(solution)/shard_map/all_to_all | solution.py:58
  307.4 5.5 %all_to_all.41 = bf16[384,3584]{1,0:T(8,128)(2,1)} reshape(bf16[64,6,3584]{2,1,0:T(8,128)(2,1)} %all-to-all-done.2) | data formatting | bytes 5505024 | tf_op jit(solution)/shard_map/all_to_all | solution.py:58
  312.9 2.7 fusion.5
  316.7 90.3 %all_to_all.54 = bf16[64,6,3584]{2,1,0:T(8,128)(2,1)} all-to-all(bf16[64,6,3584]{2,1,0:T(8,128)(2,1)S(1)} %bitcast.39), channel_id=1, replica_groups=mesh['dp'=8,'expert'=64] {'expert'}, dimensions={0} | all-to-all | bytes 5505024 | tf_op jit(solution)/shard_map/all_to_all | solution.py:59
  407.0 5.5 %all_to_all.44 = bf16[384,3584]{1,0:T(8,128)(2,1)} reshape(bf16[64,6,3584]{2,1,0:T(8,128)(2,1)} %all_to_all.54) | data formatting | bytes 5505024 | tf_op jit(solution)/shard_map/all_to_all | solution.py:59
  412.5 2.6 convolution_convert_fusion.1
  422.6 5.4 %all_to_all.45 = bf16[64,6,3584]{2,1,0:T(8,128)(2,1)} reshape(bf16[384,3584]{1,0:T(8,128)(2,1)} %fusion) | data formatting | bytes 5505024 | tf_op jit(solution)/shard_map/all_to_all | solution.py:91
  428.0 5.6 %all-to-all-start.4 = ((bf16[64,6,3584]{2,1,0:T(8,128)(2,1)}), bf16[64,6,3584]{2,1,0:T(8,128)(2,1)}, u32[]{:S(2)}, u32[]{:S(2)}) async-start(bf16[64,6,3584]{2,1,0:T(8,128)(2,1)} %all_to_all.45), calls=%async_computation.4 | async-start | bytes 7340032 | tf_op jit(solution)/shard_map/all_to_all | solution.py:91
  435.3 4.5 copy.35
  443.4 3.4 fusion.1
  446.8 71.8 %all-to-all-done.4 = bf16[64,6,3584]{2,1,0:T(8,128)(2,1)} async-done(((bf16[64,6,3584]{2,1,0:T(8,128)(2,1)}), bf16[64,6,3584]{2,1,0:T(8,128)(2,1)}, u32[]{:S(2)}, u32[]{:S(2)}) %all-to-all-start.4) | async-done | bytes 2752544 | tf_op jit(solution)/shard_map/all_to_all | solution.py:91
  518.5 5.6 %all_to_all.47 = bf16[384,3584]{1,0:T(8,128)(2,1)} reshape(bf16[64,6,3584]{2,1,0:T(8,128)(2,1)} %all-to-all-done.4) | data formatting | bytes 5505024 | tf_op jit(solution)/shard_map/all_to_all | solution.py:91
  524.1 3.4 convolution_convert_fusion.4
  (78 shorter events, 24.3 us)
Async XLA Ops:
  7.2 305.7 %copy-start = (bf16[128,3584]{1,0:T(8,128)(2,1)S(1)}, bf16[128,3584]{1,0:T(8,128)(2,1)}, u32[]{:S(2)}) copy-start(bf16[128,3584]{1,0:T(8,128)(2,1)} %param.8) | copy-start | bytes 2752516
  16.6 2.9 copy-start.7
  20.2 95.7 %copy-start.8 = (bf16[448,128]{1,0:T(8,128)(2,1)S(1)}, bf16[448,128]{1,0:T(8,128)(2,1)}, u32[]{:S(2)}) copy-start(bf16[448,128]{1,0:T(8,128)(2,1)} %param.13) | copy-start | bytes 344068
  115.9 11.4 %copy-start.9 = (bf16[448,128]{1,0:T(8,128)(2,1)S(1)}, bf16[448,128]{1,0:T(8,128)(2,1)}, u32[]{:S(2)}) copy-start(bf16[448,128]{1,0:T(8,128)(2,1)} %param.11) | copy-start | bytes 344068
  115.9 54.6 %copy-start.10 = (bf16[448,128]{1,0:T(8,128)(2,1)S(1)}, bf16[448,128]{1,0:T(8,128)(2,1)}, u32[]{:S(2)}) copy-start(bf16[448,128]{1,0:T(8,128)(2,1)} %param.12) | copy-start | bytes 344068
  116.9 89.4 %all-to-all-start.1 = ((bf16[8,448,128]{2,1,0:T(8,128)(2,1)}), bf16[8,448,128]{2,1,0:T(8,128)(2,1)}, u32[]{:S(2)}, u32[]{:S(2)}) async-start(bf16[8,448,128]{2,1,0:T(8,128)(2,1)} %stack.2), calls=%async_computation.1 | async-start | bytes 1835008 | tf_op jit(solution)/shard_map/all_to_all | solution.py:43
  196.9 8.6 %copy-start.5 = (bf16[3584,128]{1,0:T(8,128)(2,1)}, bf16[3584,128]{1,0:T(8,128)(2,1)S(1)}, u32[]{:S(2)}) copy-start(bf16[3584,128]{1,0:T(8,128)(2,1)S(1)} %all_gather.7) | copy-start | bytes 2752516
  202.7 2.8 copy-start.2
  215.4 7.0 %copy-start.11 = (f32[128,8]{0,1:T(8,128)S(1)}, f32[128,8]{0,1:T(8,128)}, u32[]{:S(2)}) copy-start(f32[128,8]{0,1:T(8,128)} %param.10) | copy-start | bytes 12292
  215.4 91.9 %all-to-all-start.2 = ((bf16[64,6,3584]{2,1,0:T(8,128)(2,1)}), bf16[64,6,3584]{2,1,0:T(8,128)(2,1)}, u32[]{:S(2)}, u32[]{:S(2)}) async-start(bf16[64,6,3584]{2,1,0:T(8,128)(2,1)} %all_to_all.39), calls=%async_computation.2 | async-start | bytes 7340032 | tf_op jit(solution)/shard_map/all_to_all | solution.py:58
  412.5 2.6 copy-start.4
  415.1 2.2 copy-start.3
  418.9 1.2 copy-start.6
  428.0 90.6 %all-to-all-start.4 = ((bf16[64,6,3584]{2,1,0:T(8,128)(2,1)}), bf16[64,6,3584]{2,1,0:T(8,128)(2,1)}, u32[]{:S(2)}, u32[]{:S(2)}) async-start(bf16[64,6,3584]{2,1,0:T(8,128)(2,1)} %all_to_all.45), calls=%async_computation.4 | async-start | bytes 7340032 | tf_op jit(solution)/shard_map/all_to_all | solution.py:91
  433.6 93.9 %reduce-scatter.4.cloned.1.call-start = ((), (), s32[]{:S(2)}) async-start(), calls=%async_computation.6 | async-start | bytes 3096576
  518.5 10.7 %copy-start.1 = (bf16[128,3584]{1,0:T(8,128)(2,1)S(1)}, bf16[128,3584]{1,0:T(8,128)(2,1)}, u32[]{:S(2)}) copy-start(bf16[128,3584]{1,0:T(8,128)(2,1)} %param.8) | copy-start | bytes 2752516
Sparse Core Ops, SparseCore 0:
  440.0 46.8 reduce-scatter.3
